TPU v7x, 32 devices: a whole 2x2x4 slice. The times are simulated.
32 devices in a mesh: gr: 4 (over z), gc: 8 (over y, x, core).
Axes of the slice: x: 2, y: 2, z: 4, core: 2. Of those that a mesh axis runs over, the one named last changes fastest.
Arguments:
- student: bfloat16 [4096, 1024], P(('gr', 'gc')), may hold values from -500 to 500
- teacher: bfloat16 [4096, 1024], P(('gr', 'gc')), may hold values from -500 to 500
Outputs:
- student_grad: float32 [4096, 1024], P(('gr', 'gc'))
All inputs are finite; a program needn't handle non-finite values.
Results may differ from a plain program's by a relative error of at most 0.0085.
Values may be sent and summed in bfloat16 or wider, within the bound.
No kernel may reach another device: no remote copies, remote signals or barrier semaphores. Data moves between devices by JAX's collectives and lax.ppermute only.
A program may use at most 64 MiB of HBM per device.

v0:
```python
import jax
import jax.numpy as jnp
from jax import lax
from jax.sharding import PartitionSpec as P

D = 1024


def unit_rows(embedded):
    values = embedded.astype(jnp.float32)
    inverse_rms = lax.rsqrt(jnp.mean(values * values, axis=-1, keepdims=True) + 1e-06)
    unit = (values * inverse_rms * D ** (-0.5)).astype(jnp.bfloat16)
    return (unit, inverse_rms)


def mismatch_of(piece_s, piece_t, other_s, other_t):
    sim_student = lax.dot_general(
        piece_s, other_s, (((1,), (1,)), ((), ())), preferred_element_type=jnp.float32
    )
    sim_teacher = lax.dot_general(
        piece_t, other_t, (((1,), (1,)), ((), ())), preferred_element_type=jnp.float32
    )
    stretch = 0.5 * D**0.5
    return jnp.tanh(stretch * (sim_student - sim_teacher)).astype(jnp.bfloat16)


def local(student, teacher):
    unit_s, inv_s = unit_rows(student)
    unit_t, inv_t = unit_rows(teacher)
    column_s, column_t = (
        lax.all_gather(unit_s, "gr", axis=0, tiled=True),
        lax.all_gather(unit_t, "gr", axis=0, tiled=True),
    )
    piece_s = lax.all_gather(unit_s, "gc", axis=0, tiled=True)
    piece_t = lax.all_gather(unit_t, "gc", axis=0, tiled=True)
    mismatch = mismatch_of(piece_s, piece_t, column_s, column_t)
    carried = lax.dot_general(
        mismatch, piece_s, (((0,), (0,)), ((), ())), preferred_element_type=jnp.float32
    )
    pull = lax.psum_scatter(carried, "gr", scatter_dimension=0, tiled=True)
    unit_float = unit_s.astype(jnp.float32)
    radial = jnp.sum(unit_float * pull, axis=-1, keepdims=True)
    total_rows = unit_s.shape[0] * lax.axis_size("gr") * lax.axis_size("gc")
    factor = 12.0 * (D / total_rows) ** 0.5
    return factor * inv_s * (pull - radial * unit_float)


def solution(mesh):
    in_specs = (P(("gr", "gc"), None), P(("gr", "gc"), None))
    out_specs = P(("gr", "gc"), None)
    return jax.shard_map(local, mesh=mesh, in_specs=in_specs, out_specs=out_specs, check_vma=False)
```

profile of v0, /device:TPU:0, one launch (start us, length us, event | category | flops | bytes accessed | tf_op | source)
XLA Modules:
  0.0 187.9 jit_solution(5423686631979588535)
XLA Ops:
  6.5 0.0 all-gather.7.cloned.1.call-start
  6.5 1.1 fusion.1
  7.6 1.8 fusion.3
  9.4 0.0 all-gather.7.cloned.1.call-update
  9.4 0.0 all-gather.5.cloned.1.call-start
  9.5 0.7 all-gather.5.cloned.1.call-update
  10.2 0.0 all-gather.11.cloned.1.call-start
  10.2 1.1 fusion.4
  11.3 1.8 fusion.6
  13.1 0.0 all-gather.11.cloned.1.call-update
  13.2 0.0 all-gather.9.cloned.1.call-start
  13.2 0.5 all-gather.9.cloned.1.call-update
  13.8 0.0 reduce-scatter.2.cloned.1.call-start
  13.8 26.5 %all-gather.7.cloned.1.call-done = bf16[512,1024]{1,0:T(8,128)(2,1)} async-done(((bf16[128,1024]{1,0:T(8,128)(2,1)}), bf16[512,1024]{1,0:T(8,128)(2,1)}) %all-gather.7.cloned.1.call-update) | async-done | bytes 1048592 | tf_op jit(solution)/shard_map/all_gather | solution.py:31
  40.3 29.1 %all-gather.5.cloned.1.call-done = bf16[1024,1024]{1,0:T(8,128)(2,1)} async-done(((bf16[128,1024]{1,0:T(8,128)(2,1)}), bf16[1024,1024]{1,0:T(8,128)(2,1)}) %all-gather.5.cloned.1.call-update) | async-done | bytes 2097168 | tf_op jit(solution)/shard_map/all_gather | solution.py:34
  69.4 0.0 copy-start.1
  69.4 4.6 %fusion.11 = f32[1024,512]{1,0:T(8,128)} fusion(bf16[1024,1024]{1,0:T(8,128)(2,1)} %all-gather.5.cloned.1.call-done, bf16[512,1024]{1,0:T(8,128)(2,1)} %all-gather.7.cloned.1.call-done), kind=kOutput, calls=%fused_computation.21 | convolution fusion | flops 1073741824 | bytes 5242880 | tf_op jit(solution)/shard_map/dot_general | solution.py:17
  74.0 25.0 %all-gather.11.cloned.1.call-done = bf16[512,1024]{1,0:T(8,128)(2,1)} async-done(((bf16[128,1024]{1,0:T(8,128)(2,1)}), bf16[512,1024]{1,0:T(8,128)(2,1)}) %all-gather.11.cloned.1.call-update) | async-done | bytes 1048592 | tf_op jit(solution)/shard_map/all_gather | solution.py:32
  99.0 28.9 %all-gather.9.cloned.1.call-done = bf16[1024,1024]{1,0:T(8,128)(2,1)} async-done(((bf16[128,1024]{1,0:T(8,128)(2,1)}), bf16[1024,1024]{1,0:T(8,128)(2,1)}) %all-gather.9.cloned.1.call-update) | async-done | bytes 2097168 | tf_op jit(solution)/shard_map/all_gather | solution.py:35
  127.9 0.0 copy-done.1
  127.9 6.4 %fusion = f32[512,1024]{1,0:T(8,128)} fusion(bf16[1024,1024]{1,0:T(8,128)(2,1)S(1)} %copy-done.1, f32[1024,512]{1,0:T(8,128)} %fusion.11, bf16[1024,1024]{1,0:T(8,128)(2,1)} %all-gather.9.cloned.1.call-done, bf16[512,1024]{1,0:T(8,128)(2,1)} %all-gather.11.cloned.1.call-done), kind=kOutput, calls=%fused_computation.1 | convolution fusion | flops 2149056512 | bytes 9437184 | tf_op jit(solution)/shard_map/dot_general | solution.py:37
  134.3 0.0 copy-start
  134.3 0.0 reduce-scatter.2.cloned.1.call-update
  134.3 43.8 %reduce-scatter.2.cloned.1.call-done = f32[128,1024]{1,0:T(8,128)} async-done(((f32[512,1024]{1,0:T(8,128)}), f32[128,1024]{1,0:T(8,128)}) %reduce-scatter.2.cloned.1.call-update) | async-done | bytes 524304 | tf_op jit(solution)/shard_map/reduce_scatter | solution.py:40
  178.1 0.0 copy-done
  178.1 1.3 fusion.7
  179.3 2.1 %fusion.9 = f32[128,1024]{1,0:T(8,128)} fusion(f32[128,1024]{1,0:T(8,128)} %reduce-scatter.2.cloned.1.call-done, f32[128]{0:T(128)S(1)} %fusion.7, f32[128]{0:T(128)S(1)} %get-tuple-element.5, f32[128]{0:T(128)S(1)} %get-tuple-element.6, bf16[128,1024]{1,0:T(8,128)(2,1)S(1)} %copy-done), kind=kLoop, calls=%fused_computation.16 | loop fusion | flops 1048576 | bytes 1312256 | tf_op jit(solution)/shard_map/mul | solution.py:45
  (2 shorter events, 0.0 us)
Async XLA Ops:
  6.5 33.8 %all-gather.7.cloned.1.call-start = ((), (), s32[]{:S(2)}) async-start(), calls=%async_computation.2 | async-start | bytes 1310720 | tf_op jit(solution)/shard_map/all_gather | solution.py:31
  9.4 59.9 %all-gather.5.cloned.1.call-start = ((), (), s32[]{:S(2)}) async-start(), calls=%async_computation.1 | async-start | bytes 2359296 | tf_op jit(solution)/shard_map/all_gather | solution.py:34
  10.2 88.8 %all-gather.11.cloned.1.call-start = ((), (), s32[]{:S(2)}) async-start(), calls=%async_computation.4 | async-start | bytes 1310720 | tf_op jit(solution)/shard_map/all_gather | solution.py:32
  13.2 114.7 %all-gather.9.cloned.1.call-start = ((), (), s32[]{:S(2)}) async-start(), calls=%async_computation.3 | async-start | bytes 2359296 | tf_op jit(solution)/shard_map/all_gather | solution.py:35
  13.8 164.3 %reduce-scatter.2.cloned.1.call-start = ((), (), s32[]{:S(2)}) async-start(), calls=%async_computation.5 | async-start | bytes 2621440 | tf_op jit(solution)/shard_map/reduce_scatter | solution.py:40
  69.4 58.5 %copy-start.1 = (bf16[1024,1024]{1,0:T(8,128)(2,1)S(1)}, bf16[1024,1024]{1,0:T(8,128)(2,1)}, u32[]{:S(2)}) copy-start(bf16[1024,1024]{1,0:T(8,128)(2,1)} %all-gather.5.cloned.1.call-done) | copy-start | bytes 6291460
  134.3 43.8 %copy-start = (bf16[128,1024]{1,0:T(8,128)(2,1)S(1)}, bf16[128,1024]{1,0:T(8,128)(2,1)}, u32[]{:S(2)}) copy-start(bf16[128,1024]{1,0:T(8,128)(2,1)} %param.2) | copy-start | bytes 786436
Sparse Core Ops, SparseCore 0:
  9.6 30.6 all-gather.6
  42.2 27.1 all-gather.4
  71.0 27.9 all-gather.10
  100.7 27.1 all-gather.8
  134.4 43.5 reduce-scatter.1
where the time goes:
time: 188 us
  waiting for transfers between devices  155 us (82%)
  between operations  13.1 us (7%)
  matrix products  11 us (6%)
  other arithmetic  9.13 us (5%)
    reduce_scatter x1, waiting for transfers between devices, local(): pull = lax.psum_scatter(carried, 'gr', scatter_dimension=0, tiled=True)  43.8 us
    all_gather x1, waiting for transfers between devices, local(): piece_s = lax.all_gather(unit_s, 'gc', axis=0, tiled=True)  29.1 us
    all_gather x1, waiting for transfers between devices, local(): piece_t = lax.all_gather(unit_t, 'gc', axis=0, tiled=True)  28.9 us
    all_gather x1, waiting for transfers between devices, local(): lax.all_gather(unit_s, 'gr', axis=0, tiled=True)  26.5 us
    all_gather x1, waiting for transfers between devices, local(): lax.all_gather(unit_t, 'gr', axis=0, tiled=True)  25 us
    dot_general x1, matrix products, local(): lax.dot_general(mismatch, piece_s, (((0,), (0,)), ((), ())), preferred_el...  6.36 us
    dot_general x1, matrix products, mismatch_of(): lax.dot_general(piece_s, other_s, (((1,), (1,)), ((), ())), preferred_ele...  4.6 us
  transfers between devices with their start and end apart: 5, of which 5 were waited for; matrix products, arithmetic and copies ran while one was open for 4% of the time, Pallas kernels for 0%

commit v1 on v0

--- a/solution.py
+++ b/solution.py
@@ -4,6 +4,20 @@
 from jax.sharding import PartitionSpec as P
 
 D = 1024
+
+
+def set_wait(q_in, along_axis):
+    shaped = lax.axis_size(along_axis)
+    current_value = lax.axis_index(along_axis)
+    local_part, lower = (shaped, current_value)
+    even, res = (q_in, 1)
+    while res < local_part:
+        b_now = lax.ppermute(even, along_axis, [(j, j ^ res) for j in range(local_part)])
+        base_arr = jnp.concatenate([even, b_now], axis=0)
+        upper = jnp.concatenate([b_now, even], axis=0)
+        even = jnp.where(lower & res == 0, base_arr, upper)
+        res = 2 * res
+    return even
 
 
 def unit_rows(embedded):
@@ -32,7 +46,7 @@
         lax.all_gather(unit_t, "gr", axis=0, tiled=True),
     )
     piece_s = lax.all_gather(unit_s, "gc", axis=0, tiled=True)
-    piece_t = lax.all_gather(unit_t, "gc", axis=0, tiled=True)
+    piece_t = set_wait(unit_t, "gc")
     mismatch = mismatch_of(piece_s, piece_t, column_s, column_t)
     carried = lax.dot_general(
         mismatch, piece_s, (((0,), (0,)), ((), ())), preferred_element_type=jnp.float32

time: 188 us -> 161 us (0.86)
  waiting for transfers between devices: 155 us -> 123 us
  starting transfers between devices: 0.16 us -> 5.43 us
    all_gather x1 -> x0, waiting for transfers between devices: 28.9 us -> none  [local(): piece_t = lax.all_gather(unit_t, 'gc', axis=0, tiled=True)]
    all_gather x1, waiting for transfers between devices: 26.5 us -> 8.56 us  [local(): lax.all_gather(unit_s, 'gr', axis=0, tiled=True)]
    ppermute x0 -> x3, waiting for transfers between devices: none -> 13.3 us  [set_wait(): lax.ppermute(even, along_axis, [(j, j ^ res) for j in range(local_part)])]
    ppermute x0 -> x3, starting transfers between devices: none -> 5.3 us  [set_wait(): lax.ppermute(even, along_axis, [(j, j ^ res) for j in range(local_part)])]
    all_gather x1, waiting for transfers between devices: 29.1 us -> 31.8 us  [local(): piece_s = lax.all_gather(unit_s, 'gc', axis=0, tiled=True)]
  transfers between devices with their start and end apart: 5 -> 7, of which waited for: 5 -> 6; matrix products, arithmetic and copies ran while one was open for 4% -> 4% of each run, Pallas kernels for 0% -> 0%
where the time goes in v1:
time: 161 us
  waiting for transfers between devices  123 us (76%)
  between operations  13.2 us (8%)
  matrix products  10.8 us (7%)
  other arithmetic  9 us (6%)
  starting transfers between devices  5.43 us (3%)
    reduce_scatter x1, waiting for transfers between devices, local(): pull = lax.psum_scatter(carried, 'gr', scatter_dimension=0, tiled=True)  43.1 us
    all_gather x1, waiting for transfers between devices, local(): piece_s = lax.all_gather(unit_s, 'gc', axis=0, tiled=True)  31.8 us
    all_gather x1, waiting for transfers between devices, local(): lax.all_gather(unit_t, 'gr', axis=0, tiled=True)  25.1 us
    ppermute x3, waiting for transfers between devices, set_wait(): lax.ppermute(even, along_axis, [(j, j ^ res) for j in range(local_part)])  13.3 us
    all_gather x1, waiting for transfers between devices, local(): lax.all_gather(unit_s, 'gr', axis=0, tiled=True)  8.56 us
    dot_general x1, matrix products, local(): lax.dot_general(mismatch, piece_s, (((0,), (0,)), ((), ())), preferred_el...  6.31 us
    ppermute x3, starting transfers between devices, set_wait(): lax.ppermute(even, along_axis, [(j, j ^ res) for j in range(local_part)])  5.3 us
    dot_general x1, matrix products, mismatch_of(): lax.dot_general(piece_s, other_s, (((1,), (1,)), ((), ())), preferred_ele...  4.45 us
  transfers between devices with their start and end apart: 7, of which 6 were waited for; matrix products, arithmetic and copies ran while one was open for 4% of the time, Pallas kernels for 0%

profile of v1, /device:TPU:0, one launch (start us, length us, event | category | flops | bytes accessed | tf_op | source)
XLA Modules:
  0.0 161.0 jit_solution(4322727501613220378)
XLA Ops:
  6.5 0.0 all-gather.6.cloned.1.call-start
  6.5 1.1 fusion.9
  7.6 1.8 %fusion.11 = bf16[128,1024]{1,0:T(8,128)(2,1)} fusion(bf16[128,1024]{1,0:T(8,128)(2,1)} %param.2, f32[128]{0:T(128)S(1)} %get-tuple-element.6), kind=kLoop, calls=%fused_computation.20 | loop fusion | flops 524288 | bytes 524800 | tf_op jit(solution)/shard_map/convert_element_type | solution.py:26
  9.4 0.0 all-gather.6.cloned.1.call-update
  9.4 0.0 all-gather.4.cloned.1.call-start
  9.5 0.7 all-gather.4.cloned.1.call-update
  10.2 0.0 all-gather.8.cloned.1.call-start
  10.2 1.1 fusion.12
  11.3 1.1 fusion.14
  12.4 0.0 copy-start.1
  12.4 0.6 collective-permute-start
  13.0 1.2 collective-permute-done
  14.2 0.1 maximum_select_fusion.7
  14.3 2.9 %collective-permute-start.1 = (bf16[256,1024]{1,0:T(8,128)(2,1)S(1)}, bf16[256,1024]{1,0:T(8,128)(2,1)S(1)}, u32[]{:S(2)}, u32[]{:S(2)}) collective-permute-start(bf16[256,1024]{1,0:T(8,128)(2,1)S(1)} %maximum_select_fusion.7), channel_id=1, source_target_pairs={{0,2},{1,3},{2,0},{3,1},{4,6},{5,7},{6,4},{7,5},{8,10},{9,11},{10,... | collective-permute-start | bytes 1572872 | tf_op jit(solution)/shard_map/ppermute | solution.py:15
  17.2 0.0 copy-done.1
  17.2 0.0 all-gather.8.cloned.1.call-update
  17.2 0.0 reduce-scatter.2.cloned.1.call-start
  17.3 12.1 %collective-permute-done.1 = bf16[256,1024]{1,0:T(8,128)(2,1)S(1)} collective-permute-done((bf16[256,1024]{1,0:T(8,128)(2,1)S(1)}, bf16[256,1024]{1,0:T(8,128)(2,1)S(1)}, u32[]{:S(2)}, u32[]{:S(2)}) %collective-permute-start.1) | collective-permute-done | bytes 524320 | tf_op jit(solution)/shard_map/ppermute | solution.py:15
  29.4 0.5 maximum_select_fusion.6
  29.9 1.8 %collective-permute-start.2 = (bf16[512,1024]{1,0:T(8,128)(2,1)S(1)}, bf16[512,1024]{1,0:T(8,128)(2,1)S(1)}, u32[]{:S(2)}, u32[]{:S(2)}) collective-permute-start(bf16[512,1024]{1,0:T(8,128)(2,1)S(1)} %maximum_select_fusion.6), channel_id=1, source_target_pairs={{0,4},{1,5},{2,6},{3,7},{4,0},{5,1},{6,2},{7,3},{8,12},{9,13},{10,... | collective-permute-start | bytes 3145736 | tf_op jit(solution)/shard_map/ppermute | solution.py:15
  31.7 8.6 %all-gather.6.cloned.1.call-done = bf16[512,1024]{1,0:T(8,128)(2,1)} async-done(((bf16[128,1024]{1,0:T(8,128)(2,1)}), bf16[512,1024]{1,0:T(8,128)(2,1)}) %all-gather.6.cloned.1.call-update) | async-done | bytes 1048592 | tf_op jit(solution)/shard_map/all_gather | solution.py:45
  40.3 31.8 %all-gather.4.cloned.1.call-done = bf16[1024,1024]{1,0:T(8,128)(2,1)} async-done(((bf16[128,1024]{1,0:T(8,128)(2,1)}), bf16[1024,1024]{1,0:T(8,128)(2,1)}) %all-gather.4.cloned.1.call-update) | async-done | bytes 2097168 | tf_op jit(solution)/shard_map/all_gather | solution.py:48
  72.1 4.5 %fusion.21 = f32[1024,512]{1,0:T(8,128)} fusion(bf16[1024,1024]{1,0:T(8,128)(2,1)} %all-gather.4.cloned.1.call-done, bf16[512,1024]{1,0:T(8,128)(2,1)} %all-gather.6.cloned.1.call-done), kind=kOutput, calls=%fused_computation.33 | convolution fusion | flops 1073741824 | bytes 5242880 | tf_op jit(solution)/shard_map/dot_general | solution.py:31
  76.5 25.1 %all-gather.8.cloned.1.call-done = bf16[512,1024]{1,0:T(8,128)(2,1)} async-done(((bf16[128,1024]{1,0:T(8,128)(2,1)}), bf16[512,1024]{1,0:T(8,128)(2,1)}) %all-gather.8.cloned.1.call-update) | async-done | bytes 1048592 | tf_op jit(solution)/shard_map/all_gather | solution.py:46
  101.7 0.0 collective-permute-done.2
  101.7 6.3 %fusion.7 = f32[512,1024]{1,0:T(8,128)} fusion(bf16[1024,1024]{1,0:T(8,128)(2,1)} %all-gather.4.cloned.1.call-done, f32[1024,512]{1,0:T(8,128)} %fusion.21, bf16[512,1024]{1,0:T(8,128)(2,1)} %all-gather.8.cloned.1.call-done, bf16[512,1024]{1,0:T(8,128)(2,1)S(1)} %collective-permute-done.2, bf16[512,1024]{1,0:T(8,128)(2,1)S(1)} %maximum_select_fusion.6, ...), kind=kOutput, calls=%fused_computation.9 | convolution fusion | flops 2158493696 | bytes 9437185 | tf_op jit(solution)/shard_map/dot_general | solution.py:51
  108.0 0.0 copy-start
  108.0 0.0 reduce-scatter.2.cloned.1.call-update
  108.0 43.1 %reduce-scatter.2.cloned.1.call-done = f32[128,1024]{1,0:T(8,128)} async-done(((f32[512,1024]{1,0:T(8,128)}), f32[128,1024]{1,0:T(8,128)}) %reduce-scatter.2.cloned.1.call-update) | async-done | bytes 524304 | tf_op jit(solution)/shard_map/reduce_scatter | solution.py:54
  151.2 0.0 copy-done
  151.2 1.3 fusion.15
  152.4 2.1 %fusion.17 = f32[128,1024]{1,0:T(8,128)} fusion(f32[128,1024]{1,0:T(8,128)} %reduce-scatter.2.cloned.1.call-done, f32[128]{0:T(128)S(1)} %fusion.15, f32[128]{0:T(128)S(1)} %get-tuple-element.5, f32[128]{0:T(128)S(1)} %get-tuple-element.6, bf16[128,1024]{1,0:T(8,128)(2,1)S(1)} %copy-done), kind=kLoop, calls=%fused_computation.26 | loop fusion | flops 1048576 | bytes 1312256 | tf_op jit(solution)/shard_map/mul | solution.py:59
  (2 shorter events, 0.0 us)
Async XLA Ops:
  6.5 33.8 %all-gather.6.cloned.1.call-start = ((), (), s32[]{:S(2)}) async-start(), calls=%async_computation.2 | async-start | bytes 1310720 | tf_op jit(solution)/shard_map/all_gather | solution.py:45
  9.4 62.7 %all-gather.4.cloned.1.call-start = ((), (), s32[]{:S(2)}) async-start(), calls=%async_computation.1 | async-start | bytes 2359296 | tf_op jit(solution)/shard_map/all_gather | solution.py:48
  10.2 91.5 %all-gather.8.cloned.1.call-start = ((), (), s32[]{:S(2)}) async-start(), calls=%async_computation.3 | async-start | bytes 1310720 | tf_op jit(solution)/shard_map/all_gather | solution.py:46
  12.4 4.8 %copy-start.1 = (bf16[128,1024]{1,0:T(8,128)(2,1)}, bf16[128,1024]{1,0:T(8,128)(2,1)S(1)}, u32[]{:S(2)}) copy-start(bf16[128,1024]{1,0:T(8,128)(2,1)S(1)} %fusion.14) | copy-start | bytes 786436
  12.4 1.7 %collective-permute-start = (bf16[128,1024]{1,0:T(8,128)(2,1)S(1)}, bf16[128,1024]{1,0:T(8,128)(2,1)S(1)}, u32[]{:S(2)}, u32[]{:S(2)}) collective-permute-start(bf16[128,1024]{1,0:T(8,128)(2,1)S(1)} %fusion.14), channel_id=1, source_target_pairs={{0,1},{1,0},{2,3},{3,2},{4,5},{5,4},{6,7},{7,6},{8,9},{9,8},{10,11... | collective-permute-start | bytes 786440 | tf_op jit(solution)/shard_map/ppermute | solution.py:15
  14.3 15.1 %collective-permute-start.1 = (bf16[256,1024]{1,0:T(8,128)(2,1)S(1)}, bf16[256,1024]{1,0:T(8,128)(2,1)S(1)}, u32[]{:S(2)}, u32[]{:S(2)}) collective-permute-start(bf16[256,1024]{1,0:T(8,128)(2,1)S(1)} %maximum_select_fusion.7), channel_id=1, source_target_pairs={{0,2},{1,3},{2,0},{3,1},{4,6},{5,7},{6,4},{7,5},{8,10},{9,11},{10,... | collective-permute-start | bytes 1572872 | tf_op jit(solution)/shard_map/ppermute | solution.py:15
  17.2 133.9 %reduce-scatter.2.cloned.1.call-start = ((), (), s32[]{:S(2)}) async-start(), calls=%async_computation.4 | async-start | bytes 2621440 | tf_op jit(solution)/shard_map/reduce_scatter | solution.py:54
  29.9 71.8 %collective-permute-start.2 = (bf16[512,1024]{1,0:T(8,128)(2,1)S(1)}, bf16[512,1024]{1,0:T(8,128)(2,1)S(1)}, u32[]{:S(2)}, u32[]{:S(2)}) collective-permute-start(bf16[512,1024]{1,0:T(8,128)(2,1)S(1)} %maximum_select_fusion.6), channel_id=1, source_target_pairs={{0,4},{1,5},{2,6},{3,7},{4,0},{5,1},{6,2},{7,3},{8,12},{9,13},{10,... | collective-permute-start | bytes 3145736 | tf_op jit(solution)/shard_map/ppermute | solution.py:15
  108.0 43.2 %copy-start = (bf16[128,1024]{1,0:T(8,128)(2,1)S(1)}, bf16[128,1024]{1,0:T(8,128)(2,1)}, u32[]{:S(2)}) copy-start(bf16[128,1024]{1,0:T(8,128)(2,1)} %param.2) | copy-start | bytes 786436
Sparse Core Ops, SparseCore 0:
  9.6 30.6 all-gather.5
  42.2 29.8 all-gather.3
  73.7 27.9 all-gather.7
  108.1 42.9 reduce-scatter.1
